TPU v7x, 512 devices: a whole 4x8x8 slice. The times are simulated.
512 devices in a mesh: rows: 32 (over y_hi, z, core), cols: 16 (over y_lo, x).
Axes of the slice: x: 4, y: 8 (y_hi: 2, y_lo: 4; y = y_hi * 4 + y_lo), z: 8, core: 2. Of those that a mesh axis runs over, the one named last changes fastest.
Arguments:
- jac: bfloat16 [32768, 1024], P(('rows', 'cols')), may hold values from -0.29882812 to 0.29882812
- panel_jac: bfloat16 [32768, 512], P(('rows', 'cols')), may hold values from -6 to 6
- weights: float32 [32768], P(('rows', 'cols')), may hold values from 0.1 to 1
- tile_lists: int32 [1024, 4], P(('rows', 'cols')), may hold values from 0 to 95, as said below
- tile_masks: int32 [1024, 4], P(('rows', 'cols')), may hold values from 0 to 1
- tile_order: int32 [96], replicated, may hold values from 0 to 95, as said below
- factor_inverse: float32 [512, 512], replicated, as said below
Outputs:
- panel_factor: float32 [96, 256, 512], P('cols', 'rows')
Inputs may be any that keep to these rules, and one draw needn't show every extreme that they name: `tile_order`: a permutation of 0 to 95. `tile_lists`: the 4 tiles of one row block are distinct; among the active slots of one device's 2 row blocks, at most 2 name tiles whose positions i share i // 6; in every draw every device has 2 such slots for one and the same position range. `factor_inverse`: lower triangular with a positive diagonal.
All inputs are finite; a program needn't handle non-finite values.
Results may differ from a plain program's by a relative error of at most 0.0029.
Values may be sent and summed in bfloat16 or wider, within the bound.
A program may use at most 64 MiB of HBM per device.

v0:
```python
import jax
import jax.numpy as jnp
from jax import lax
from jax.sharding import PartitionSpec as P


def tile_positions(tile_lists, tile_order):
    tile_count = tile_order.shape[0]
    matches = tile_lists[:, :, None] == tile_order[None, None, :]
    return jnp.sum(jnp.where(matches, jnp.arange(tile_count, dtype=jnp.int32), 0), axis=2)


def apply_inverse(tiles, factor_inverse):
    return jnp.einsum("ntp,qp->ntq", tiles, factor_inverse, precision=lax.Precision.HIGHEST)


def local(jac, panel_jac, weights, tile_lists, tile_masks, tile_order, factor_inverse):
    block_count, slot_count = tile_lists.shape
    block_rows = jac.shape[0] // block_count
    tile_width = jac.shape[1] // slot_count
    panel_width = panel_jac.shape[1]
    owners = lax.axis_size("cols")
    per_owner = tile_order.shape[0] // owners
    positions = tile_positions(tile_lists, tile_order)
    weighted = (weights[:, None] * panel_jac).astype(jnp.bfloat16)
    first_place = lax.axis_index("cols") * per_owner
    jac_piece = lax.all_gather(jac, "cols", axis=0, tiled=True)
    weighted_piece = lax.all_gather(weighted, "cols", axis=0, tiled=True)
    place_piece = lax.all_gather(positions, "cols", axis=0, tiled=True)
    mask_piece = lax.all_gather(tile_masks, "cols", axis=0, tiled=True)
    blocks_here = place_piece.shape[0]
    local_place = place_piece - first_place
    chosen = (
        (local_place[:, :, None] == jnp.arange(per_owner, dtype=jnp.int32))
        & (mask_piece[:, :, None] == 1)
    ).astype(jnp.bfloat16)
    columns = jac_piece.reshape(blocks_here, block_rows, slot_count, tile_width)
    mixed_tiles = jnp.einsum(
        "bkn,brkt->brnt", chosen, columns, preferred_element_type=jnp.float32
    ).astype(jnp.bfloat16)
    panels = weighted_piece.reshape(blocks_here, block_rows, panel_width)
    gram_tiles = jnp.einsum(
        "brnt,brp->ntp", mixed_tiles, panels, preferred_element_type=jnp.float32
    )
    reduced = lax.psum_scatter(gram_tiles, "rows", scatter_dimension=1, tiled=True)
    return apply_inverse(reduced, factor_inverse)


def solution(mesh):
    in_specs = (
        P(("rows", "cols"), None),
        P(("rows", "cols"), None),
        P(("rows", "cols")),
        P(("rows", "cols"), None),
        P(("rows", "cols"), None),
        P(),
        P(),
    )
    out_specs = P("cols", "rows", None)
    return jax.shard_map(local, mesh=mesh, in_specs=in_specs, out_specs=out_specs, check_vma=False)
```

profile of v0, /device:TPU:1, one launch (start us, length us, event | category | flops | bytes accessed | tf_op | source)
XLA Modules:
  0.0 336.5 jit_solution(16019776710534135513)
XLA Ops:
  6.5 0.0 copy-start
  6.5 0.0 all-gather.5.cloned.1.call-start
  6.5 0.7 all-gather.5.cloned.1.call-update
  7.3 0.0 all-gather.7.cloned.1.call-start
  7.3 1.5 multiply_convert_fusion
  8.9 0.0 all-gather.7.cloned.1.call-update
  8.9 0.0 reduce-scatter.2.cloned.1.call-start
  8.9 37.6 %all-gather.1 = s32[16,2,4]{2,1,0:T(2,128)S(1)} all-gather(s32[1,2,4]{2,1,0:T(2,128)} %bitcast.27), channel_id=1, replica_groups=mesh['rows'=32,'cols'=16] {'cols'}, dimensions={0}, use_global_device_ids=true | all-gather | bytes 544 | tf_op jit(solution)/shard_map/all_gather | solution.py:30
  46.5 0.1 copy.18
  46.6 0.1 copy.24
  46.7 0.9 select_reduce_fusion
  47.6 31.6 %all-gather = s32[16,2,4]{2,1,0:T(2,128)S(1)} all-gather(s32[1,2,4]{2,1,0:T(2,128)S(1)} %bitcast.26), channel_id=1, replica_groups=mesh['rows'=32,'cols'=16] {'cols'}, dimensions={0}, use_global_device_ids=true | all-gather | bytes 544 | tf_op jit(solution)/shard_map/all_gather | solution.py:29
  79.3 12.2 %all-gather.5.cloned.1.call-done = bf16[1024,1024]{1,0:T(8,128)(2,1)} async-done(((bf16[64,1024]{1,0:T(8,128)(2,1)}), bf16[1024,1024]{1,0:T(8,128)(2,1)}) %all-gather.5.cloned.1.call-update) | async-done | bytes 2097168 | tf_op jit(solution)/shard_map/all_gather | solution.py:27
  91.5 3.3 reshape.12
  94.8 3.2 convert_bitcast_fusion
  98.0 77.0 %all-gather.7.cloned.1.call-done = bf16[1024,512]{1,0:T(8,128)(2,1)} async-done(((bf16[64,512]{1,0:T(8,128)(2,1)}), bf16[1024,512]{1,0:T(8,128)(2,1)}) %all-gather.7.cloned.1.call-update) | async-done | bytes 1048592 | tf_op jit(solution)/shard_map/all_gather | solution.py:28
  175.1 6.0 %fusion.2 = f32[6,256,512]{2,1,0:T(8,128)} fusion(bf16[32,32,512,1]{2,1,0,3:T(8,128)(2,1)} %bitcast.28, bf16[32,32,6,256]{3,2,1,0:T(8,128)(2,1)} %convert_bitcast_fusion), kind=kOutput, calls=%fused_computation.3 | convolution fusion | flops 1610612736 | bytes 7340032 | tf_op jit(solution)/shard_map/brnt,brp->ntp/dot_general | solution.py:42
  181.1 0.0 reduce-scatter.2.cloned.1.call-update
  181.2 146.2 %reduce-scatter.2.cloned.1.call-done = f32[6,8,512]{2,1,0:T(8,128)} async-done(((f32[6,256,512]{2,1,0:T(8,128)}), f32[6,8,512]{2,1,0:T(8,128)}) %reduce-scatter.2.cloned.1.call-update) | async-done | bytes 98320 | tf_op jit(solution)/shard_map/reduce_scatter | solution.py:45
  327.3 0.0 copy-done
  327.3 2.6 fusion.5
  (3 shorter events, 0.0 us)
Async XLA Ops:
  6.5 320.8 %copy-start = (f32[512,512]{1,0:T(8,128)S(1)}, f32[512,512]{1,0:T(8,128)}, u32[]{:S(2)}) copy-start(f32[512,512]{1,0:T(8,128)} %param.13) | copy-start | bytes 3145732
  6.5 84.9 %all-gather.5.cloned.1.call-start = ((), (), s32[]{:S(2)}) async-start(), calls=%async_computation.1 | async-start | bytes 2228224 | tf_op jit(solution)/shard_map/all_gather | solution.py:27
  7.3 167.8 %all-gather.7.cloned.1.call-start = ((), (), s32[]{:S(2)}) async-start(), calls=%async_computation.2 | async-start | bytes 1114112 | tf_op jit(solution)/shard_map/all_gather | solution.py:28
  8.9 318.5 %reduce-scatter.2.cloned.1.call-start = ((), (), s32[]{:S(2)}) async-start(), calls=%async_computation.3 | async-start | bytes 3244032 | tf_op jit(solution)/shard_map/reduce_scatter | solution.py:45
Sparse Core Ops, SparseCore 0:
  9.4 82.0 all-gather.4
  93.6 81.4 all-gather.6
  181.3 146.0 reduce-scatter.1
where the time goes:
time: 341 us; the launch traced here: 336 us
  waiting for transfers between devices  236 us (69%)
  blocking collectives  69.2 us (20%)
  between operations  13.1 us (4%)
  matrix products  11.9 us (3%)
  local copies, waits for them, and re-layouts  3.56 us (1%)
    reduce_scatter x1, waiting for transfers between devices, local(): lax.psum_scatter(gram_tiles, 'rows', scatter_dimension=1, tiled=True)  146 us
    all_gather x1, waiting for transfers between devices, local(): weighted_piece = lax.all_gather(weighted, 'cols', axis=0, tiled=True)  77 us
    all_gather x1, blocking collectives, local(): mask_piece = lax.all_gather(tile_masks, 'cols', axis=0, tiled=True)  37.6 us
    all_gather x1, blocking collectives, local(): place_piece = lax.all_gather(positions, 'cols', axis=0, tiled=True)  31.6 us
    all_gather x1, waiting for transfers between devices, local(): jac_piece = lax.all_gather(jac, 'cols', axis=0, tiled=True)  12.2 us
  transfers between devices with their start and end apart: 3, of which 3 were waited for; matrix products, arithmetic and copies ran while one was open for 3% of the time, Pallas kernels for 0%

commit v1 on v0

v1 whole, which is shorter than its diff:
```python
import functools

import jax
import jax.numpy as jnp
from jax import lax
from jax.experimental import pallas as pl
from jax.experimental.pallas import tpu as pltpu
from jax.sharding import PartitionSpec as P

MESH = pl.DeviceIdType.MESH
F32, BF16 = jnp.float32, jnp.bfloat16
X, YL, YH, Z, H = 4, 4, 2, 8, 2
ZH, Y = Z * H, YH * YL
KT, RB, NB, PER = 4, 32, 2, 6
ROWS, TILE, PANEL = NB * RB, 256, 512
M8 = TILE // (YH * ZH)
M = YH * M8
Q = PANEL // X
BT = X * NB
SL = KT * BT
NT = X * YL * PER
RS = M8 * X * PER


def kernel(
    jac, panel, weights, lists, masks, order, finv_hbm, out,
    ws, wk, jm, jx, px, finv, fhi, flo, bd, phi, plo, gy, ysend, yrecv, red, fs, fx,
    s_wx, r_wx, s_jz, r_jz, s_pz, r_pz, s_jx, r_jx, s_px, r_px,
    s_rp, r_rp, s_rm, r_rm, s_sb, r_sb, s_y, r_y, s_f, r_f, s_fin,
):
    ri, ci = lax.axis_index("rows"), lax.axis_index("cols")
    yh, zh = ri // ZH, ri % ZH
    z, h = zh // H, zh % H
    yl, x = ci // X, ci % X
    y = yh * YL + yl

    def at_x(d):
        return (ri, yl * X + (x + d) % X)

    def at_zh(d):
        return (yh * ZH + (zh + d) % ZH, ci)

    def at_z(d):
        return (yh * ZH + ((z + d) % Z) * H + h, ci)

    def at_y(d):
        other = (y + d) % Y
        return ((other // YL) * ZH + zh, (other % YL) * X + x)

    sibling = (yh * ZH + z * H + (1 - h), ci)

    def send(src, dst, s, r, to):
        copy = pltpu.make_async_remote_copy(src, dst, s, r, device_id=to, device_id_type=MESH)
        copy.start()

    def arrived(ref, sem):
        pltpu.make_async_copy(ref, ref, sem).wait()

    fin_copy = pltpu.make_async_copy(finv_hbm, finv, s_fin)
    fin_copy.start()
    barrier = pltpu.get_barrier_semaphore()

    def greet(n, where):
        def one(d, carry):
            pl.semaphore_signal(barrier, inc=1, device_id=where(d), device_id_type=MESH)
            return carry

        lax.fori_loop(1, n, one, 0)

    greet(X, at_x)
    greet(ZH, at_zh)
    greet(Y, at_y)

    eye = lax.broadcasted_iota(jnp.int32, (ROWS, ROWS), 0) == lax.broadcasted_iota(jnp.int32, (ROWS, ROWS), 1)
    wcol = jnp.sum(jnp.where(eye, jnp.broadcast_to(weights[...], (ROWS, ROWS)), 0.0), axis=1, keepdims=True)
    for q in range(X):
        ws[q] = (wcol * panel[:, q * Q : (q + 1) * Q].astype(F32)).astype(BF16)
    wk[zh, x] = ws[x]

    turned = []
    for k in range(KT):
        both = jnp.concatenate(
            [jac[:, k * TILE + half * 128 : k * TILE + half * 128 + 128].astype(F32) for half in range(YH)], axis=0
        )
        turned.append(both.T.reshape(ZH, M8, YH * ROWS))
    jm[...] = jnp.concatenate(turned, axis=1).astype(BF16)
    jx[x, zh] = jm[zh]

    lane = lax.broadcasted_iota(jnp.int32, (1, 128), 1)
    ids = order[...]
    place = lax.broadcasted_iota(jnp.int32, (1, NT), 1).astype(F32) + 1.0
    base = (zh % 4) * SL + x * NB
    note = jnp.zeros((1, 128), F32)
    for b in range(NB):
        for k in range(KT):
            hit = jnp.sum(jnp.where(ids == lists[b, k], place, 0.0), axis=1, keepdims=True)
            hit = hit * masks[b, k].astype(F32)
            note = note + jnp.where(lane == base + k * BT + b, hit, 0.0)
    px[x, zh] = note

    pl.semaphore_wait(barrier, X - 1 + ZH - 1 + Y - 1)

    for d in range(1, X):
        send(ws.at[(x + d) % X], wk.at[zh, x], s_wx, r_wx, at_x(d))

    def spread(d, carry):
        send(jm.at[(zh + d) % ZH], jx.at[x, zh], s_jz, r_jz, at_zh(d))
        send(px.at[x, zh], px.at[x, zh], s_pz, r_pz, at_zh(d))
        return carry

    lax.fori_loop(1, ZH, spread, 0)

    arrived(wk.at[zh, pl.ds(0, X - 1)], r_wx)
    send(wk.at[zh], wk.at[zh], s_rp.at[0], r_rp.at[0], at_z(1))
    send(wk.at[zh], wk.at[zh], s_rm.at[0], r_rm.at[0], at_z(Z - 1))
    send(wk.at[zh], wk.at[zh], s_sb.at[0], r_sb.at[0], sibling)

    arrived(jx.at[x, pl.ds(0, ZH - 1)], r_jz)
    arrived(px.at[x, pl.ds(0, ZH - 1)], r_pz)
    for d in range(1, X):
        send(jx.at[x], jx.at[x], s_jx, r_jx, at_x(d))
        send(px.at[x], px.at[x], s_px, r_px, at_x(d))

    up, down = Z // 2, Z // 2 - 1
    for s in range(1, up + 1):
        mine = wk.at[((z + Z - s) % Z) * H + h]
        arrived(mine, r_rp.at[s - 1])
        if s < up:
            send(mine, mine, s_rp.at[s], r_rp.at[s], at_z(1))
        send(mine, mine, s_sb.at[s], r_sb.at[s], sibling)
        if s <= down:
            mine = wk.at[((z + s) % Z) * H + h]
            arrived(mine, r_rm.at[s - 1])
            if s < down:
                send(mine, mine, s_rm.at[s], r_rm.at[s], at_z(Z - 1))
            send(mine, mine, s_sb.at[up + s], r_sb.at[up + s], sibling)

    fin_copy.wait()
    full = finv[...]
    high = full.astype(BF16)
    fhi[...] = high
    flo[...] = (full - high.astype(F32)).astype(BF16)

    arrived(jx.at[pl.ds(0, X - 1)], r_jx)
    arrived(px.at[pl.ds(0, X - 1)], r_px)
    for s in range(Z):
        arrived(wk.at[0], r_sb.at[s])

    low_lanes = lax.broadcasted_iota(jnp.int32, (KT * M8, 128), 1) < ROWS
    own_block = (lax.broadcasted_iota(jnp.int32, (BT, X * ROWS), 1) // RB) == lax.broadcasted_iota(
        jnp.int32, (BT, X * ROWS), 0
    )

    def product(t, carry):
        parts = [jx[i, t].astype(F32) for i in range(X)]
        swapped = [pltpu.roll(v, ROWS, 1) for v in parts]
        for half in range(YH):
            if half == 0:
                tiles = [jnp.where(low_lanes, parts[i], swapped[i + 1]) for i in range(0, X, 2)]
            else:
                tiles = [jnp.where(low_lanes, swapped[i], parts[i + 1]) for i in range(0, X, 2)]
            rows = jnp.concatenate(tiles, axis=1)
            for m in range(M8):
                for k in range(KT):
                    row = jnp.broadcast_to(rows[k * M8 + m : k * M8 + m + 1, :], (BT, X * ROWS))
                    at = (half * M8 + m) * SL + k * BT
                    bd[at : at + BT, :] = jnp.where(own_block, row, 0.0)
        terms = jnp.dot(
            bd[...].astype(BF16), wk[t].reshape(X * ROWS, Q), preferred_element_type=F32
        )
        top = terms.astype(BF16)
        rest = (terms - top.astype(F32)).astype(BF16)
        where = pl.ds(pl.multiple_of(t * SL, SL), SL)
        phi[:, where, :] = top.reshape(M, SL, Q)
        plo[:, where, :] = rest.reshape(M, SL, Q)
        return carry

    lax.fori_loop(0, ZH, product, 0)

    notes = []
    for g in range(ZH // 4):
        total = jnp.zeros((1, 128), F32)
        for i in range(X):
            for t in range(4):
                total = total + px[i, g * 4 + t]
        notes.append(total)
    slot_place = jnp.concatenate(notes, axis=1)
    wanted = lax.broadcasted_iota(jnp.int32, (NT, ZH * SL), 0).astype(F32) + 1.0
    chosen = jnp.where(wanted == slot_place, 1.0, 0.0).astype(BF16)

    for half in range(YH):
        for m in range(M8):
            here = half * M8 + m
            gram = jnp.dot(chosen, phi[here], preferred_element_type=F32) + jnp.dot(
                chosen, plo[here], preferred_element_type=F32
            )
            for low in range(YL):
                gy[half * YL + low, m * X * PER : (m + 1) * X * PER, :] = gram[low * X * PER : (low + 1) * X * PER, :]
    for i in range(Y):
        ysend[i] = gy[i].astype(BF16)

    for d in range(1, Y):
        send(ysend.at[(y + d) % Y], yrecv.at[d - 1], s_y, r_y, at_y(d))
    arrived(yrecv, r_y)
    total = gy[y]
    for d in range(Y - 1):
        total = total + yrecv[d].astype(F32)
    red[...] = total
    for i in range(X):
        for j in range(PER):
            fs[i, j] = red[pl.ds(i * PER + j, M8, stride=X * PER), :]
    fx[x] = fs[x]
    for d in range(1, X):
        send(fs.at[(x + d) % X], fx.at[x], s_f, r_f, at_x(d))
    arrived(fx.at[pl.ds(0, X - 1)], r_f)
    gram = jnp.concatenate([fx[i].reshape(PER * M8, Q) for i in range(X)], axis=1)
    ghi = gram.astype(BF16)
    glo = (gram - ghi.astype(F32)).astype(BF16)

    def times(a, b):
        return lax.dot_general(a, b[...], (((1,), (1,)), ((), ())), preferred_element_type=F32)

    out[...] = (times(ghi, fhi) + (times(ghi, flo) + times(glo, fhi))).reshape(PER, M8, PANEL)

    arrived(ws.at[pl.ds(0, X - 1)], s_wx)
    arrived(jm.at[pl.ds(0, ZH - 1)], s_jz)
    arrived(px.at[x, pl.ds(0, ZH - 1)], s_pz)
    arrived(jx.at[pl.ds(0, X - 1)], s_jx)
    arrived(px.at[pl.ds(0, X - 1)], s_px)
    for s in range(up):
        arrived(wk.at[0], s_rp.at[s])
    for s in range(down):
        arrived(wk.at[0], s_rm.at[s])
    for s in range(Z):
        arrived(wk.at[0], s_sb.at[s])
    arrived(yrecv, s_y)
    arrived(fx.at[pl.ds(0, X - 1)], s_f)


def local(jac, panel_jac, weights, tile_lists, tile_masks, tile_order, factor_inverse):
    vmem, smem = pl.BlockSpec(memory_space=pltpu.VMEM), pl.BlockSpec(memory_space=pltpu.SMEM)
    dma = pltpu.SemaphoreType.DMA
    return pl.pallas_call(
        kernel,
        out_shape=jax.ShapeDtypeStruct((PER, M8, PANEL), F32),
        in_specs=[vmem, vmem, vmem, smem, smem, vmem, pl.BlockSpec(memory_space=pl.ANY)],
        out_specs=vmem,
        scratch_shapes=[
            pltpu.VMEM((X, ROWS, Q), BF16),
            pltpu.VMEM((ZH, X, ROWS, Q), BF16),
            pltpu.VMEM((ZH, KT * M8, YH * ROWS), BF16),
            pltpu.VMEM((X, ZH, KT * M8, YH * ROWS), BF16),
            pltpu.VMEM((X, ZH, 1, 128), F32),
            pltpu.VMEM((PANEL, PANEL), F32),
            pltpu.VMEM((PANEL, PANEL), BF16),
            pltpu.VMEM((PANEL, PANEL), BF16),
            pltpu.VMEM((M * SL, X * ROWS), F32),
            pltpu.VMEM((M, ZH * SL, Q), BF16),
            pltpu.VMEM((M, ZH * SL, Q), BF16),
            pltpu.VMEM((Y, RS, Q), F32),
            pltpu.VMEM((Y, RS, Q), BF16),
            pltpu.VMEM((Y - 1, RS, Q), BF16),
            pltpu.VMEM((RS, Q), F32),
            pltpu.VMEM((X, PER, M8, Q), F32),
            pltpu.VMEM((X, PER, M8, Q), F32),
            *[dma(()) for _ in range(10)],
            dma((Z // 2,)), dma((Z // 2,)), dma((Z // 2,)), dma((Z // 2,)), dma((Z,)), dma((Z,)),
            *[dma(()) for _ in range(5)],
        ],
        compiler_params=pltpu.CompilerParams(
            collective_id=0, has_side_effects=True, vmem_limit_bytes=40 * 1024 * 1024
        ),
    )(jac, panel_jac, weights[None, :], tile_lists, tile_masks, tile_order[None, :], factor_inverse)


def solution(mesh):
    in_specs = (
        P(("rows", "cols"), None),
        P(("rows", "cols"), None),
        P(("rows", "cols")),
        P(("rows", "cols"), None),
        P(("rows", "cols"), None),
        P(),
        P(),
    )
    out_specs = P("cols", "rows", None)
    return jax.shard_map(local, mesh=mesh, in_specs=in_specs, out_specs=out_specs, check_vma=False)
```

time: 341 us -> 60.8 us (0.18); the launches traced: 336 us -> 60.6 us
  waiting for transfers between devices: 236 us -> 0 us
  blocking collectives: 69.2 us -> 0 us
  Pallas kernels: 0 us -> 56.2 us
  between operations: 13.1 us -> 0.03 us
  matrix products: 11.9 us -> 0 us
    reduce_scatter x1 -> x0, waiting for transfers between devices: 146 us -> none  [local(): lax.psum_scatter(gram_tiles, 'rows', scatter_dimension=1, tiled=True)]
    all_gather x2 -> x0, waiting for transfers between devices: 89.2 us -> none  [the longest x1 77 us: local(): weighted_piece = lax.all_gather(weighted, 'cols', axis=0, tiled=True)]
    all_gather x2 -> x0, blocking collectives: 69.2 us -> none  [the longest x1 37.6 us: local(): mask_piece = lax.all_gather(tile_masks, 'cols', axis=0, tiled=True)]
    pallas_call x0 -> x1, Pallas kernels: none -> 56.2 us  [local(): pl.pallas_call(kernel, out_shape=jax.ShapeDtypeStruct((PER, M8, PANEL), F...]
    dot_general x3 -> x0, matrix products: 11.9 us -> none  [the longest x1 6.04 us: local(): jnp.einsum('brnt,brp->ntp', mixed_tiles, panels, preferred_element_type=j...]
    unnamed x2 -> x15, local copies, waits for them, and re-layouts: 0.01 us -> 4.31 us
  transfers between devices with their start and end apart: 3 -> 0, of which waited for: 3 -> 0; matrix products, arithmetic and copies ran while one was open for 3% -> 0% of each run, Pallas kernels for 0% -> 0%
where the time goes in v1:
time: 60.8 us; the launch traced here: 60.6 us
  Pallas kernels  56.2 us (92%)
  local copies, waits for them, and re-layouts  4.31 us (7%)
    pallas_call x1, Pallas kernels, local(): pl.pallas_call(kernel, out_shape=jax.ShapeDtypeStruct((PER, M8, PANEL), F...  56.2 us
    unnamed x15, local copies, waits for them, and re-layouts  4.31 us

profile of v1, /device:TPU:1, one launch (start us, length us, event | category | flops | bytes accessed | tf_op | source)
XLA Modules:
  0.0 60.6 jit_solution(11996071812596537193)
XLA Ops:
  0.0 0.0 copy-start.4
  0.0 0.0 copy-start.6
  0.0 0.0 copy-start.3
  0.0 0.0 copy-start.5
  0.0 0.7 %copy-done.4 = s32[2,4]{1,0:T(2,128)S(1)} copy-done((s32[2,4]{1,0:T(2,128)S(1)}, s32[2,4]{1,0:T(2,128)}, u32[]{:S(2)}) %copy-start.4) | copy-done | bytes 56
  0.7 0.0 copy-done.6
  0.7 0.0 copy-done.3
  0.7 0.0 copy-done.5
  0.7 0.0 copy-start
  0.7 1.2 %copy-done = f32[512,512]{1,0:T(8,128)S(1)} copy-done((f32[512,512]{1,0:T(8,128)S(1)}, f32[512,512]{1,0:T(8,128)}, u32[]{:S(2)}) %copy-start) | copy-done | bytes 1048600
  1.9 0.0 copy-start.1
  1.9 0.9 %copy-done.1 = bf16[64,1024]{1,0:T(8,128)(2,1)S(1)} copy-done((bf16[64,1024]{1,0:T(8,128)(2,1)S(1)}, bf16[64,1024]{1,0:T(8,128)(2,1)}, u32[]{:S(2)}) %copy-start.1) | copy-done | bytes 131096
  2.8 0.0 copy-start.2
  2.8 0.8 %copy-done.2 = bf16[64,512]{1,0:T(8,128)(2,1)S(1)} copy-done((bf16[64,512]{1,0:T(8,128)(2,1)S(1)}, bf16[64,512]{1,0:T(8,128)(2,1)}, u32[]{:S(2)}) %copy-start.2) | copy-done | bytes 65560
  3.7 56.2 %shard_map.73 = f32[6,8,512]{2,1,0:T(8,128)S(1)} custom-call(bf16[64,1024]{1,0:T(8,128)(2,1)S(1)} %copy-done.1, bf16[64,512]{1,0:T(8,128)(2,1)S(1)} %copy-done.2, f32[1,64]{1,0:T(1,128)S(1)} %bitcast.2, s32[2,4]{1,0:T(2,128)S(1)} %copy-done.3, s32[2,4]{1,0:T(2,128)S(1)} %copy-done.4, s32[1,96]{1,0:T(1,128)S(1)} %bitcast.3, f32[512,512]{1,0:T(8,128)S(1)} %copy-done), custom_call_target="tpu_custom_call" | custom-call | tf_op jit(solution)/shard_map/pallas_call | solution.py:243
  59.9 0.6 %copy.9 = f32[6,8,512]{2,1,0:T(8,128)} copy(f32[6,8,512]{2,1,0:T(8,128)S(1)} %shard_map.73) | data formatting | bytes 196608
Async XLA Ops:
  0.0 0.7 %copy-start.4 = (s32[2,4]{1,0:T(2,128)S(1)}, s32[2,4]{1,0:T(2,128)}, u32[]{:S(2)}) copy-start(s32[2,4]{1,0:T(2,128)} %masks.1) | copy-start | bytes 100
  0.0 0.7 %copy-start.6 = (s32[96]{0:T(128)S(1)}, s32[96]{0:T(128)}, u32[]{:S(2)}) copy-start(s32[96]{0:T(128)} %param.12) | copy-start | bytes 1156
  0.0 0.7 %copy-start.3 = (s32[2,4]{1,0:T(2,128)S(1)}, s32[2,4]{1,0:T(2,128)}, u32[]{:S(2)}) copy-start(s32[2,4]{1,0:T(2,128)} %lists.1) | copy-start | bytes 100
  0.0 0.7 %copy-start.5 = (f32[64]{0:T(128)S(1)}, f32[64]{0:T(128)}, u32[]{:S(2)}) copy-start(f32[64]{0:T(128)} %param.9) | copy-start | bytes 772
  0.7 1.2 %copy-start = (f32[512,512]{1,0:T(8,128)S(1)}, f32[512,512]{1,0:T(8,128)}, u32[]{:S(2)}) copy-start(f32[512,512]{1,0:T(8,128)} %finv_hbm.1) | copy-start | bytes 3145732
  1.9 0.9 %copy-start.1 = (bf16[64,1024]{1,0:T(8,128)(2,1)S(1)}, bf16[64,1024]{1,0:T(8,128)(2,1)}, u32[]{:S(2)}) copy-start(bf16[64,1024]{1,0:T(8,128)(2,1)} %jac.1) | copy-start | bytes 393220
  2.8 0.8 %copy-start.2 = (bf16[64,512]{1,0:T(8,128)(2,1)S(1)}, bf16[64,512]{1,0:T(8,128)(2,1)}, u32[]{:S(2)}) copy-start(bf16[64,512]{1,0:T(8,128)(2,1)} %panel.1) | copy-start | bytes 196612

commit v2 on v1

v2 whole, which is shorter than its diff:
```python
import functools

import jax
import jax.numpy as jnp
from jax import lax
from jax.experimental import pallas as pl
from jax.experimental.pallas import tpu as pltpu
from jax.sharding import PartitionSpec as P

MESH = pl.DeviceIdType.MESH
F32, BF16 = jnp.float32, jnp.bfloat16
X, YL, YH, Z, H = 4, 4, 2, 8, 2
ZH, Y = Z * H, YH * YL
KT, RB, NB, PER = 4, 32, 2, 6
ROWS, TILE, PANEL = NB * RB, 256, 512
M8 = TILE // (YH * ZH)
M = YH * M8
Q = PANEL // X
BT = X * NB
SL = KT * BT
NT = X * YL * PER


def kernel(
    jac_hbm, panel_hbm, weights_hbm, lists_hbm, masks_hbm, order_hbm, finv_hbm, out,
    jac, panel, weights, lists, masks, order,
    ws, wk, jm, jx, px, finv, fhi, flo, bd, phi, plo, gy, ysend, yrecv,
    s_in, s_wx, r_wx, s_jz, r_jz, s_pz, r_pz, s_jx, r_jx, s_px, r_px,
    s_h, r_near, r_far, r_half, s_sb, r_sb, s_y, r_y,
):
    inputs = [
        pltpu.make_async_copy(src, dst, s_in.at[i])
        for i, (src, dst) in enumerate([
            (panel_hbm, panel), (weights_hbm, weights), (jac_hbm, jac), (lists_hbm, lists),
            (masks_hbm, masks), (order_hbm, order), (finv_hbm, finv),
        ])
    ]
    for copy in inputs:
        copy.start()

    ri, ci = lax.axis_index("rows"), lax.axis_index("cols")
    yh, zh = ri // ZH, ri % ZH
    z, h = zh // H, zh % H
    yl, x = ci // X, ci % X
    y = yh * YL + yl

    def at_x(d):
        return (ri, yl * X + (x + d) % X)

    def at_zh(d):
        return (yh * ZH + (zh + d) % ZH, ci)

    def at_z(d):
        return (yh * ZH + ((z + d) % Z) * H + h, ci)

    def at_yx(there, across):
        return ((there // YL) * ZH + zh, (there % YL) * X + across)

    sibling = (yh * ZH + z * H + (1 - h), ci)

    def send(src, dst, s, r, to):
        copy = pltpu.make_async_remote_copy(src, dst, s, r, device_id=to, device_id_type=MESH)
        copy.start()

    def arrived(ref, sem):
        pltpu.make_async_copy(ref, ref, sem).wait()

    barrier = pltpu.get_barrier_semaphore()

    def greet(n, where):
        def one(d, carry):
            pl.semaphore_signal(barrier, inc=1, device_id=where(d), device_id_type=MESH)
            return carry

        lax.fori_loop(1, n, one, 0)

    greet(ZH, at_zh)
    greet(Y * X, lambda d: at_yx((y + d // X) % Y, (x + d) % X))

    inputs[0].wait()
    inputs[1].wait()
    eye = lax.broadcasted_iota(jnp.int32, (ROWS, ROWS), 0) == lax.broadcasted_iota(jnp.int32, (ROWS, ROWS), 1)
    wcol = jnp.sum(jnp.where(eye, jnp.broadcast_to(weights[...], (ROWS, ROWS)), 0.0), axis=1, keepdims=True)
    for q in range(X):
        ws[q] = (wcol * panel[:, q * Q : (q + 1) * Q].astype(F32)).astype(BF16)

    pl.semaphore_wait(barrier, ZH - 1 + Y * X - 1)

    for d in range(1, X):
        send(ws.at[(x + d) % X], wk.at[zh, x], s_wx, r_wx, at_x(d))
    wk[zh, x] = ws[x]

    inputs[2].wait()
    turned = []
    for k in range(KT):
        both = jnp.concatenate(
            [jac[:, k * TILE + half * 128 : k * TILE + half * 128 + 128].astype(F32) for half in range(YH)], axis=0
        )
        turned.append(both.T.reshape(ZH, M8, YH * ROWS))
    jm[...] = jnp.concatenate(turned, axis=1).astype(BF16)

    def spread(d, carry):
        send(jm.at[(zh + d) % ZH], jx.at[x, zh], s_jz, r_jz.at[z], at_zh(d))
        return carry

    lax.fori_loop(1, ZH, spread, 0)
    jx[x, zh] = jm[zh]

    for copy in inputs[3:6]:
        copy.wait()
    lane = lax.broadcasted_iota(jnp.int32, (1, 128), 1)
    ids = order[...]
    place = lax.broadcasted_iota(jnp.int32, (1, NT), 1).astype(F32) + 1.0
    base = (zh % 4) * SL + x * NB
    note = jnp.zeros((1, 128), F32)
    for b in range(NB):
        for k in range(KT):
            hit = jnp.sum(jnp.where(ids == lists[b, k], place, 0.0), axis=1, keepdims=True)
            hit = hit * masks[b, k].astype(F32)
            note = note + jnp.where(lane == base + k * BT + b, hit, 0.0)
    px[x, zh] = note

    def tell(d, carry):
        send(px.at[x, zh], px.at[x, zh], s_pz, r_pz, at_zh(d))
        return carry

    lax.fori_loop(1, ZH, tell, 0)

    arrived(wk.at[zh, pl.ds(0, X - 1)], r_wx)
    for i, d in enumerate((2, Z - 2, 1, Z - 1)):
        send(wk.at[zh], wk.at[zh], s_h, r_near.at[i], at_z(d))
    send(wk.at[zh], wk.at[zh], s_sb, r_sb.at[z], sibling)

    def pass_jac(i, carry):
        zz = (z + (i % 2) * ((i + 1) // 2) + (1 - i % 2) * (Z - i // 2)) % Z
        mine = jx.at[x, pl.ds(zz * H, H)]

        @pl.when(i == 0)
        def _():
            arrived(jx.at[x, pl.ds(0, 1)], r_jz.at[zz])

        @pl.when(i > 0)
        def _():
            arrived(mine, r_jz.at[zz])

        for d in range(1, X):
            send(mine, mine, s_jx, r_jx.at[zz], at_x(d))
        return carry

    lax.fori_loop(0, Z, pass_jac, 0)

    arrived(px.at[x, pl.ds(0, ZH - 1)], r_pz)
    for d in range(1, X):
        send(px.at[x], px.at[x], s_px, r_px, at_x(d))

    def chunk(d):
        return wk.at[((z + d) % Z) * H + h]

    def share(d):
        send(chunk(d), chunk(d), s_sb, r_sb.at[(z + d) % Z], sibling)

    inputs[6].wait()
    full = finv[...]
    high = full.astype(BF16)
    fhi[...] = high
    flo[...] = (full - high.astype(F32)).astype(BF16)

    for i, (d, first, step) in enumerate(((Z - 2, 0, 1), (2, X // 2, Z - 1))):
        arrived(chunk(d), r_near.at[i])
        send(chunk(d), chunk(d), s_h, r_far.at[i], at_z(step))
        part = wk.at[((z + d) % Z) * H + h, pl.ds(first, X // 2)]
        send(part, part, s_h, r_half.at[i], at_z(2 * step))
        share(d)
    for i, d in enumerate((Z - 1, 1)):
        arrived(chunk(d), r_near.at[2 + i])
        share(d)

    low_lanes = lax.broadcasted_iota(jnp.int32, (KT * M8, 128), 1) < ROWS
    own_block = (lax.broadcasted_iota(jnp.int32, (BT, X * ROWS), 1) // RB) == lax.broadcasted_iota(
        jnp.int32, (BT, X * ROWS), 0
    )

    def distance(i):
        return (z + (i % 2) * ((i + 1) // 2) + (1 - i % 2) * (Z - i // 2)) % Z

    def lay_out(t, carry):
        parts = [jx[i, t].astype(F32) for i in range(X)]
        swapped = [pltpu.roll(v, ROWS, 1) for v in parts]
        for half in range(YH):
            if half == 0:
                tiles = [jnp.where(low_lanes, parts[i], swapped[i + 1]) for i in range(0, X, 2)]
            else:
                tiles = [jnp.where(low_lanes, swapped[i], parts[i + 1]) for i in range(0, X, 2)]
            rows = jnp.concatenate(tiles, axis=1)
            for m in range(M8):
                for k in range(0, KT, 2):
                    pair = [
                        jnp.where(own_block, jnp.broadcast_to(rows[r : r + 1, :], (BT, X * ROWS)), 0.0)
                        for r in (k * M8 + m, (k + 1) * M8 + m)
                    ]
                    at = (half * M8 + m) * SL + k * BT
                    bd[t, at : at + 2 * BT, :] = jnp.concatenate(pair, axis=0).astype(BF16)
        return carry

    def lay_out_pair(i, carry):
        zz = distance(i)
        arrived(jx.at[pl.ds(0, X - 1), pl.ds(zz * H, H)], r_jx.at[zz])
        return lax.fori_loop(zz * H, zz * H + H, lay_out, carry)

    def product(t, first, count):
        terms = jnp.dot(
            bd[t, first * SL : (first + count) * SL, :], wk[t].reshape(X * ROWS, Q), preferred_element_type=F32
        )
        top = terms.astype(BF16)
        rest = (terms - top.astype(F32)).astype(BF16)
        where = pl.ds(pl.multiple_of(t * SL, SL), SL)
        phi[first : first + count, where, :] = top.reshape(count, SL, Q)
        plo[first : first + count, where, :] = rest.reshape(count, SL, Q)

    def near_products(i, carry):
        zz = distance(i)
        arrived(wk.at[0], r_sb.at[zz])
        for core in range(H):
            product(zz * H + core, 0, M)
        return carry

    near = 5
    lax.fori_loop(0, near, lay_out_pair, 0)
    lax.fori_loop(0, near, near_products, 0)
    for i, d in enumerate((Z - 3, 3)):
        arrived(chunk(d), r_far.at[i])
        share(d)
    lax.fori_loop(near, Z - 1, lay_out_pair, 0)
    arrived(wk.at[0, pl.ds(0, X // 2)], r_half.at[0])
    arrived(wk.at[0, pl.ds(0, X // 2)], r_half.at[1])
    share(Z // 2)
    lay_out_pair(Z - 1, 0)

    arrived(px.at[pl.ds(0, X - 1)], r_px)
    notes = []
    for g in range(ZH // 4):
        total = jnp.zeros((1, 128), F32)
        for i in range(X):
            for t in range(4):
                total = total + px[i, g * 4 + t]
        notes.append(total)
    slot_place = jnp.concatenate(notes, axis=1)
    wanted = lax.broadcasted_iota(jnp.int32, (NT, ZH * SL), 0).astype(F32) + 1.0
    chosen = jnp.where(wanted == slot_place, 1.0, 0.0).astype(BF16)

    for half in range(YH):

        def far_products(i, carry):
            zz = distance(i)
            if half == 0:
                arrived(wk.at[0], r_sb.at[zz])
            for core in range(H):
                product(zz * H + core, half * M8, M8)
            return carry

        lax.fori_loop(near, Z, far_products, 0)
        for m in range(M8):
            here = half * M8 + m
            gram = jnp.dot(chosen, phi[here], preferred_element_type=F32) + jnp.dot(
                chosen, plo[here], preferred_element_type=F32
            )
            for low in range(YL):
                gy[low, m * X * PER : (m + 1) * X * PER, :] = gram[low * X * PER : (low + 1) * X * PER, :]
        for low in range(YL):
            for i in range(X):
                piece = [gy[low, pl.ds(i * PER + j, M8, stride=X * PER), :] for j in range(PER)]
                ysend[half * YL + low, i] = jnp.concatenate(piece, axis=0).astype(BF16)

        def deliver(n, carry):
            there, across = half * YL + (yl + n // X) % YL, (x + n) % X
            mine = (there == y) & (across == x)

            @pl.when(jnp.logical_not(mine))
            def _():
                send(ysend.at[there, across], yrecv.at[y * X + x], s_y, r_y, at_yx(there, across))

            @pl.when(mine)
            def _():
                yrecv[y * X + x] = ysend[y, x]

            return carry

        lax.fori_loop(0, YL * X, deliver, 0)

    arrived(yrecv.at[pl.ds(0, Y * X - 1)], r_y)
    quarters = []
    for i in range(X):
        total = yrecv[i].astype(F32)
        for other in range(1, Y):
            total = total + yrecv[other * X + i].astype(F32)
        quarters.append(total)
    gram = jnp.concatenate(quarters, axis=1)
    ghi = gram.astype(BF16)
    glo = (gram - ghi.astype(F32)).astype(BF16)

    def times(a, b):
        return lax.dot_general(a, b[...], (((1,), (1,)), ((), ())), preferred_element_type=F32)

    out[...] = (times(ghi, fhi) + (times(ghi, flo) + times(glo, fhi))).reshape(PER, M8, PANEL)

    arrived(ws.at[pl.ds(0, X - 1)], s_wx)
    arrived(jm.at[pl.ds(0, ZH - 1)], s_jz)
    arrived(px.at[x, pl.ds(0, ZH - 1)], s_pz)
    arrived(jx.at[pl.ds(0, X - 1)], s_jx)
    arrived(px.at[pl.ds(0, X - 1)], s_px)
    arrived(wk.at[pl.ds(0, Z - 1)], s_h)
    arrived(wk.at[pl.ds(0, Z)], s_sb)
    arrived(yrecv.at[pl.ds(0, Y * X - 1)], s_y)


def local(jac, panel_jac, weights, tile_lists, tile_masks, tile_order, factor_inverse):
    dma = pltpu.SemaphoreType.DMA
    return pl.pallas_call(
        kernel,
        out_shape=jax.ShapeDtypeStruct((PER, M8, PANEL), F32),
        in_specs=[pl.BlockSpec(memory_space=pltpu.HBM)] * 7,
        out_specs=pl.BlockSpec(memory_space=pltpu.VMEM),
        scratch_shapes=[
            pltpu.VMEM((ROWS, KT * TILE), BF16),
            pltpu.VMEM((ROWS, PANEL), BF16),
            pltpu.VMEM((1, ROWS), F32),
            pltpu.SMEM((NB, KT), jnp.int32),
            pltpu.SMEM((NB, KT), jnp.int32),
            pltpu.VMEM((1, NT), jnp.int32),
            pltpu.VMEM((X, ROWS, Q), BF16),
            pltpu.VMEM((ZH, X, ROWS, Q), BF16),
            pltpu.VMEM((ZH, KT * M8, YH * ROWS), BF16),
            pltpu.VMEM((X, ZH, KT * M8, YH * ROWS), BF16),
            pltpu.VMEM((X, ZH, 1, 128), F32),
            pltpu.VMEM((PANEL, PANEL), F32),
            pltpu.VMEM((PANEL, PANEL), BF16),
            pltpu.VMEM((PANEL, PANEL), BF16),
            pltpu.VMEM((ZH, M * SL, X * ROWS), BF16),
            pltpu.VMEM((M, ZH * SL, Q), BF16),
            pltpu.VMEM((M, ZH * SL, Q), BF16),
            pltpu.VMEM((YL, M8 * X * PER, Q), F32),
            pltpu.VMEM((Y, X, PER * M8, Q), BF16),
            pltpu.VMEM((Y * X, PER * M8, Q), BF16),
            dma((7,)), dma(()), dma(()), dma(()), dma((Z,)), dma(()), dma(()), dma(()), dma((Z,)), dma(()), dma(()),
            dma(()), dma((4,)), dma((2,)), dma((2,)), dma(()), dma((Z,)), dma(()), dma(()),
        ],
        compiler_params=pltpu.CompilerParams(
            collective_id=0, has_side_effects=True, vmem_limit_bytes=60 * 1024 * 1024
        ),
    )(jac, panel_jac, weights[None, :], tile_lists, tile_masks, tile_order[None, :], factor_inverse)


def solution(mesh):
    in_specs = (
        P(("rows", "cols"), None),
        P(("rows", "cols"), None),
        P(("rows", "cols")),
        P(("rows", "cols"), None),
        P(("rows", "cols"), None),
        P(),
        P(),
    )
    out_specs = P("cols", "rows", None)
    return jax.shard_map(local, mesh=mesh, in_specs=in_specs, out_specs=out_specs, check_vma=False)
```

time: 60.8 us -> 49.2 us (0.81)
  the two profiles are of different devices: /device:TPU:1 before, /device:TPU:56 now
where the time goes in v2:
time: 49.2 us; the launch traced here: 49 us
  Pallas kernels  47.5 us (97%)
  local copies, waits for them, and re-layouts  1.54 us (3%)
    pallas_call x1, Pallas kernels, local(): pl.pallas_call(kernel, out_shape=jax.ShapeDtypeStruct((PER, M8, PANEL), F...  47.5 us
    unnamed x1, local copies, waits for them, and re-layouts  1.54 us

profile of v2, /device:TPU:56, one launch (start us, length us, event | category | flops | bytes accessed | tf_op | source)
XLA Modules:
  0.0 49.0 jit_solution(3639525631260889944)
XLA Ops:
  0.0 47.5 %shard_map.73 = f32[6,8,512]{2,1,0:T(8,128)} custom-call(bf16[64,1024]{1,0:T(8,128)(2,1)} %jac_hbm.1, bf16[64,512]{1,0:T(8,128)(2,1)} %panel_hbm.1, f32[1,64]{1,0:T(1,128)} %bitcast.2, s32[2,4]{1,0:T(2,128)} %lists_hbm.1, s32[2,4]{1,0:T(2,128)} %masks_hbm.1, s32[1,96]{1,0:T(1,128)} %bitcast.3, f32[512,512]{1,0:T(8,128)} %finv_hbm.1), custom_call_target="tpu_custom_call" | custom-call | tf_op jit(solution)/shard_map/pallas_call | solution.py:318
  47.5 1.5 %copy.9 = f32[6,8,512]{2,1,0:T(8,128)} copy(f32[6,8,512]{2,1,0:T(8,128)} %shard_map.73) | data formatting | bytes 196608

commit v3 on v2

v3 whole, which is shorter than its diff:
```python
import functools

import jax
import jax.numpy as jnp
from jax import lax
from jax.experimental import pallas as pl
from jax.experimental.pallas import tpu as pltpu
from jax.sharding import PartitionSpec as P

MESH = pl.DeviceIdType.MESH
F32, BF16 = jnp.float32, jnp.bfloat16
X, YL, YH, Z, H = 4, 4, 2, 8, 2
ZH, Y = Z * H, YH * YL
KT, RB, NB, PER = 4, 32, 2, 6
ROWS, TILE, PANEL = NB * RB, 256, 512
M8 = TILE // (YH * ZH)
M = YH * M8
M4 = M8 // 2
Q = PANEL // X
BT = X * NB
SL = KT * BT
NT = X * YL * PER


def kernel(
    jac_hbm, panel_hbm, weights_hbm, lists_hbm, masks_hbm, order_hbm, finv_hbm, out,
    jac, panel, weights, lists, masks, order,
    ws, wk, jm, jx, px, finv, fhi, flo, bd, phi, plo, gy, ysend, yrecv, done,
    s_in, s_w, s_w0, r_w, s_jz, r_jz, s_pz, r_pz, s_jx, r_jx, s_px, r_px,
    s_h, r_far, r_half, s_sb, r_sb, s_y, r_y, ready,
):
    inputs = [
        pltpu.make_async_copy(src, dst, s_in.at[i])
        for i, (src, dst) in enumerate([
            (panel_hbm, panel), (weights_hbm, weights), (lists_hbm, lists), (masks_hbm, masks),
            (order_hbm, order), (jac_hbm, jac), (finv_hbm, finv),
        ])
    ]
    for copy in inputs:
        copy.start()

    ri, ci = lax.axis_index("rows"), lax.axis_index("cols")
    yh, zh = ri // ZH, ri % ZH
    z, h = zh // H, zh % H
    yl, x = ci // X, ci % X
    y = yh * YL + yl

    def at_xz(dx, dz):
        return (yh * ZH + ((z + dz) % Z) * H + h, yl * X + (x + dx) % X)

    def at_x(d):
        return at_xz(d, 0)

    def at_z(d):
        return at_xz(0, d)

    def at_zh(d):
        return (yh * ZH + (zh + d) % ZH, ci)

    def at_yx(there, across):
        return ((there // YL) * ZH + zh, (there % YL) * X + across)

    sibling = (yh * ZH + z * H + (1 - h), ci)

    def send(src, dst, s, r, to):
        copy = pltpu.make_async_remote_copy(src, dst, s, r, device_id=to, device_id_type=MESH)
        copy.start()

    def arrived(ref, sem):
        pltpu.make_async_copy(ref, ref, sem).wait()

    barrier = pltpu.get_barrier_semaphore()

    def greet(n, where):
        for d in range(1, n):
            pl.semaphore_signal(barrier, inc=1, device_id=where(d), device_id_type=MESH)

    for dz in (2, Z - 2, 0, 1, Z - 1):
        greet(X, lambda d: at_xz(d, dz))
    greet(ZH, at_zh)
    greet(Y, lambda d: at_yx((y + d) % Y, x))

    inputs[0].wait()
    inputs[1].wait()
    eye = lax.broadcasted_iota(jnp.int32, (ROWS, ROWS), 0) == lax.broadcasted_iota(jnp.int32, (ROWS, ROWS), 1)
    wcol = jnp.sum(jnp.where(eye, jnp.broadcast_to(weights[...], (ROWS, ROWS)), 0.0), axis=1, keepdims=True)
    for q in range(X):
        ws[q] = (wcol * panel[:, q * Q : (q + 1) * Q].astype(F32)).astype(BF16)

    for copy in inputs[2:5]:
        copy.wait()
    lane = lax.broadcasted_iota(jnp.int32, (1, 128), 1)
    ids = order[...]
    place = lax.broadcasted_iota(jnp.int32, (1, NT), 1).astype(F32) + 1.0
    base = (zh % 4) * SL + x * NB
    note = jnp.zeros((1, 128), F32)
    for b in range(NB):
        for k in range(KT):
            hit = jnp.sum(jnp.where(ids == lists[b, k], place, 0.0), axis=1, keepdims=True)
            hit = hit * masks[b, k].astype(F32)
            note = note + jnp.where(lane == base + k * BT + b, hit, 0.0)
    px[x, zh] = note

    pl.semaphore_wait(barrier, 5 * (X - 1) + ZH - 1 + Y - 1)

    def near(dz, first, sem):
        def one(dx, carry):
            send(ws.at[(x + dx) % X], wk.at[zh, x], sem, r_w.at[z], at_xz(dx, dz))
            return carry

        lax.fori_loop(first, X, one, 0)

    near(2, 0, s_w)
    near(Z - 2, 0, s_w)
    near(0, 1, s_w0)
    wk[zh, x] = ws[x]

    inputs[5].wait()
    turned = []
    for k in range(KT):
        both = [jac[:, k * TILE + i * 128 : k * TILE + i * 128 + 128].astype(F32) for i in range(YH)]
        turned.append(jnp.concatenate(both, axis=0).T)
    first_four = lax.broadcasted_iota(jnp.int32, (ZH * M8, 128), 0) % M8 < M4
    for half in range(2):
        tiles = []
        for k in range(0, KT, 2):
            if half == 0:
                tile = jnp.where(first_four, turned[k], pltpu.roll(turned[k + 1], M4, 0))
            else:
                tile = jnp.where(first_four, pltpu.roll(turned[k], ZH * M8 - M4, 0), turned[k + 1])
            tiles.append(tile.reshape(ZH, M8, 128))
        jm[half] = jnp.concatenate(tiles, axis=1).astype(BF16)

    def spread(half):
        def one(d, carry):
            send(jm.at[half, (zh + d) % ZH], jx.at[half, x, zh], s_jz.at[half], r_jz.at[half, z], at_zh(d))
            return carry

        lax.fori_loop(1, ZH, one, 0)

    spread(0)

    def tell(d, carry):
        send(px.at[x, zh], px.at[x, zh], s_pz, r_pz, at_zh(d))
        return carry

    lax.fori_loop(1, ZH, tell, 0)
    for d in range(1, Y):
        pl.semaphore_signal(ready, inc=1, device_id=at_yx((y + d) % Y, x), device_id_type=MESH)

    spread(1)
    near(1, 0, s_w)
    near(Z - 1, 0, s_w)
    for half in range(YH):
        jx[half, x, zh] = jm[half, zh]

    inputs[6].wait()
    full = finv[...]
    high = full.astype(BF16)
    fhi[...] = high
    flo[...] = (full - high.astype(F32)).astype(BF16)

    def chunk(d):
        return wk.at[((z + d) % Z) * H + h]

    def share(d):
        send(chunk(d), chunk(d), s_sb, r_sb.at[(z + d) % Z], sibling)


    for i, (d, first, step) in enumerate(((Z - 2, 0, 1), (2, X // 2, Z - 1))):
        arrived(chunk(d), r_w.at[(z + d) % Z])
        send(chunk(d), chunk(d), s_h, r_far.at[i], at_z(step))
        part = wk.at[((z + d) % Z) * H + h, pl.ds(first, X // 2)]
        send(part, part, s_h, r_half.at[i], at_z(2 * step))
        share(d)

    def distance(i):
        return (z + (i % 2) * ((i + 1) // 2) + (1 - i % 2) * (Z - i // 2)) % Z

    def pass_jac(half):
        def one(i, carry):
            zz = distance(i)
            mine = jx.at[half, x, pl.ds(zz * H, H)]

            @pl.when(i == 0)
            def _():
                arrived(jx.at[half, x, pl.ds(0, 1)], r_jz.at[half, zz])

            @pl.when(i > 0)
            def _():
                arrived(mine, r_jz.at[half, zz])

            for d in range(1, X):
                send(mine, mine, s_jx.at[half], r_jx.at[half, zz], at_x(d))
            return carry

        lax.fori_loop(0, Z, one, 0)

    pass_jac(0)
    arrived(px.at[x, pl.ds(0, ZH - 1)], r_pz)
    for d in range(1, X):
        send(px.at[x], px.at[x], s_px, r_px, at_x(d))
    arrived(wk.at[0, pl.ds(0, X - 1)], r_w.at[z])
    share(0)
    for d in (Z - 1, 1):
        arrived(chunk(d), r_w.at[(z + d) % Z])
        share(d)
    pass_jac(1)

    low_lanes = lax.broadcasted_iota(jnp.int32, (2 * M8, 128), 1) < ROWS
    own_block = (lax.broadcasted_iota(jnp.int32, (BT, X * ROWS), 1) // RB) == lax.broadcasted_iota(
        jnp.int32, (BT, X * ROWS), 0
    )

    def lay_out(half, t):
        parts = [jx[half, i, t].astype(F32) for i in range(X)]
        swapped = [pltpu.roll(v, ROWS, 1) for v in parts]
        for up in range(YH):
            if up == 0:
                tiles = [jnp.where(low_lanes, parts[i], swapped[i + 1]) for i in range(0, X, 2)]
            else:
                tiles = [jnp.where(low_lanes, swapped[i], parts[i + 1]) for i in range(0, X, 2)]
            rows = jnp.concatenate(tiles, axis=1)
            for m in range(M4):
                for k in range(0, KT, 2):
                    pair = [
                        jnp.where(own_block, jnp.broadcast_to(rows[r : r + 1, :], (BT, X * ROWS)), 0.0)
                        for r in (k * M4 + m, (k + 1) * M4 + m)
                    ]
                    at = (half * M8 + up * M4 + m) * SL + k * BT
                    bd[t, at : at + 2 * BT, :] = jnp.concatenate(pair, axis=0).astype(BF16)

    def product(half, t):
        terms = jnp.dot(
            bd[t, half * M8 * SL : (half + 1) * M8 * SL, :], wk[t].reshape(X * ROWS, Q), preferred_element_type=F32
        )
        top = terms.astype(BF16)
        rest = (terms - top.astype(F32)).astype(BF16)
        where = pl.ds(pl.multiple_of(t * SL, SL), SL)
        phi[half * M8 : (half + 1) * M8, where, :] = top.reshape(M8, SL, Q)
        plo[half * M8 : (half + 1) * M8, where, :] = rest.reshape(M8, SL, Q)

    def lay_out_pair(half):
        def one(i, carry):
            zz = distance(i)
            arrived(jx.at[half, pl.ds(0, X - 1), pl.ds(zz * H, H)], r_jx.at[half, zz])
            for core in range(H):
                lay_out(half, zz * H + core)
            return carry

        return one

    def products(half):
        def one(i, carry):
            zz = distance(i)
            if half == 0:
                arrived(wk.at[0], r_sb.at[zz])
            for core in range(H):
                product(half, zz * H + core)
            return carry

        return one

    close = 5
    lax.fori_loop(0, close, lay_out_pair(0), 0)
    lax.fori_loop(0, close, products(0), 0)
    for i, d in enumerate((Z - 3, 3)):
        arrived(chunk(d), r_far.at[i])
        share(d)
    arrived(wk.at[0, pl.ds(0, X // 2)], r_half.at[0])
    arrived(wk.at[0, pl.ds(0, X // 2)], r_half.at[1])
    share(Z // 2)
    lax.fori_loop(close, Z, lay_out_pair(0), 0)

    pl.semaphore_wait(ready, Y - 1)

    arrived(px.at[pl.ds(0, X - 1)], r_px)
    notes = []
    for g in range(ZH // 4):
        total = jnp.zeros((1, 128), F32)
        for i in range(X):
            for t in range(4):
                total = total + px[i, g * 4 + t]
        notes.append(total)
    slot_place = jnp.concatenate(notes, axis=1)
    line = lax.broadcasted_iota(jnp.int32, (NT, ZH * SL), 0)
    wanted = ((line % (YL * X)) * PER + line // (YL * X)).astype(F32) + 1.0
    chosen = jnp.where(wanted == slot_place, 1.0, 0.0).astype(BF16)

    for half in range(YH):
        if half == 0:
            lax.fori_loop(close, Z, products(0), 0)
        else:
            lax.fori_loop(0, Z, lay_out_pair(1), 0)
            lax.fori_loop(0, Z, products(1), 0)
        for up in range(YH):
            for m in range(M4):
                here = half * M8 + up * M4 + m
                gram = jnp.dot(chosen, phi[here], preferred_element_type=F32) + jnp.dot(
                    chosen, plo[here], preferred_element_type=F32
                )
                gy[up, m * NT : (m + 1) * NT, :] = gram
            for c in range(YL * X):
                ysend[half, up * YL * X + c] = gy[up, pl.ds(c, M4 * PER, stride=YL * X), :].astype(BF16)

        def deliver(n, carry):
            there, across = (y + n // X) % Y, (x + n) % X
            send(
                ysend.at[half, there * X + across], yrecv.at[half, y * X + x],
                s_y.at[half], r_y.at[half], at_yx(there, across),
            )
            return carry

        lax.fori_loop(1, Y * X, deliver, 0)
        yrecv[half, y * X + x] = ysend[half, y * X + x]

    for half in range(2):
        arrived(yrecv.at[half, pl.ds(0, Y * X - 1)], r_y.at[half])
        for i in range(X):
            total = yrecv[half, i].astype(F32)
            for other in range(1, Y):
                total = total + yrecv[half, other * X + i].astype(F32)
            done[i, half * M4 * PER : (half + 1) * M4 * PER, :] = total
    quarters = []
    for i in range(X):
        quarters.append(jnp.concatenate([done[i, pl.ds(j, M8, stride=PER), :] for j in range(PER)], axis=0))
    gram = jnp.concatenate(quarters, axis=1)
    ghi = gram.astype(BF16)
    glo = (gram - ghi.astype(F32)).astype(BF16)

    def times(a, b):
        return lax.dot_general(a, b[...], (((1,), (1,)), ((), ())), preferred_element_type=F32)

    out[...] = (times(ghi, fhi) + (times(ghi, flo) + times(glo, fhi))).reshape(PER, M8, PANEL)

    arrived(wk.at[pl.ds(0, 4)], s_w)
    arrived(wk.at[0, pl.ds(0, X - 1)], s_w0)
    for half in range(YH):
        arrived(jm.at[half, pl.ds(0, ZH - 1)], s_jz.at[half])
        arrived(jx.at[half, pl.ds(0, X - 1)], s_jx.at[half])
    arrived(px.at[x, pl.ds(0, ZH - 1)], s_pz)
    arrived(px.at[pl.ds(0, X - 1)], s_px)
    arrived(wk.at[pl.ds(0, 3)], s_h)
    arrived(wk.at[pl.ds(0, Z)], s_sb)
    for half in range(2):
        arrived(yrecv.at[half, pl.ds(0, Y * X - 1)], s_y.at[half])


def local(jac, panel_jac, weights, tile_lists, tile_masks, tile_order, factor_inverse):
    dma = pltpu.SemaphoreType.DMA
    given = (jac, panel_jac, weights[None, :], tile_lists, tile_masks, tile_order[None, :], factor_inverse)
    held = [pltpu.with_memory_space_constraint(value, pltpu.HBM) for value in given]
    return pl.pallas_call(
        kernel,
        out_shape=jax.ShapeDtypeStruct((PER, M8, PANEL), F32),
        in_specs=[pl.BlockSpec(memory_space=pltpu.HBM)] * 7,
        out_specs=pl.BlockSpec(memory_space=pltpu.VMEM),
        scratch_shapes=[
            pltpu.VMEM((ROWS, KT * TILE), BF16),
            pltpu.VMEM((ROWS, PANEL), BF16),
            pltpu.VMEM((1, ROWS), F32),
            pltpu.SMEM((NB, KT), jnp.int32),
            pltpu.SMEM((NB, KT), jnp.int32),
            pltpu.VMEM((1, NT), jnp.int32),
            pltpu.VMEM((X, ROWS, Q), BF16),
            pltpu.VMEM((ZH, X, ROWS, Q), BF16),
            pltpu.VMEM((YH, ZH, 2 * M8, 2 * ROWS), BF16),
            pltpu.VMEM((YH, X, ZH, 2 * M8, 2 * ROWS), BF16),
            pltpu.VMEM((X, ZH, 1, 128), F32),
            pltpu.VMEM((PANEL, PANEL), F32),
            pltpu.VMEM((PANEL, PANEL), BF16),
            pltpu.VMEM((PANEL, PANEL), BF16),
            pltpu.VMEM((ZH, M * SL, X * ROWS), BF16),
            pltpu.VMEM((M, ZH * SL, Q), BF16),
            pltpu.VMEM((M, ZH * SL, Q), BF16),
            pltpu.VMEM((YH, M4 * NT, Q), F32),
            pltpu.VMEM((2, Y * X, M4 * PER, Q), BF16),
            pltpu.VMEM((2, Y * X, M4 * PER, Q), BF16),
            pltpu.VMEM((X, M8 * PER, Q), F32),
            dma((7,)), dma(()), dma(()), dma((Z,)), dma((YH,)), dma((YH, Z)), dma(()), dma(()),
            dma((YH,)), dma((YH, Z)), dma(()), dma(()),
            dma(()), dma((2,)), dma((2,)), dma(()), dma((Z,)), dma((2,)), dma((2,)), pltpu.SemaphoreType.REGULAR,
        ],
        compiler_params=pltpu.CompilerParams(
            collective_id=0, has_side_effects=True, vmem_limit_bytes=48 * 1024 * 1024
        ),
    )(*held)


def solution(mesh):
    in_specs = (
        P(("rows", "cols"), None),
        P(("rows", "cols"), None),
        P(("rows", "cols")),
        P(("rows", "cols"), None),
        P(("rows", "cols"), None),
        P(),
        P(),
    )
    out_specs = P("cols", "rows", None)
    return jax.shard_map(local, mesh=mesh, in_specs=in_specs, out_specs=out_specs, check_vma=False)
```

time: 49.2 us -> 46.6 us (0.947)
  the two profiles are of different devices: /device:TPU:56 before, /device:TPU:1 now
where the time goes in v3:
time: 46.6 us; the launch traced here: 46.5 us
  Pallas kernels  45.9 us (98%)
  local copies, waits for them, and re-layouts  0.64 us (1%)
    pallas_call x1, Pallas kernels, local(): pl.pallas_call(kernel, out_shape=jax.ShapeDtypeStruct((PER, M8, PANEL), F...  45.9 us

profile of v3, /device:TPU:1, one launch (start us, length us, event | category | flops | bytes accessed | tf_op | source)
XLA Modules:
  0.0 46.5 jit_solution(4750762382633932848)
XLA Ops:
  0.0 45.9 %shard_map.73 = f32[6,8,512]{2,1,0:T(8,128)S(1)} custom-call(bf16[64,1024]{1,0:T(8,128)(2,1)} %jac_hbm.1, bf16[64,512]{1,0:T(8,128)(2,1)} %panel_hbm.1, f32[1,64]{1,0:T(1,128)} %bitcast.2, s32[2,4]{1,0:T(2,128)} %lists_hbm.1, s32[2,4]{1,0:T(2,128)} %masks_hbm.1, s32[1,96]{1,0:T(1,128)} %bitcast.3, f32[512,512]{1,0:T(8,128)} %finv_hbm.1), custom_call_target="tpu_custom_call" | custom-call | tf_op jit(solution)/shard_map/pallas_call | solution.py:353
  45.9 0.6 %copy.9 = f32[6,8,512]{2,1,0:T(8,128)} copy(f32[6,8,512]{2,1,0:T(8,128)S(1)} %shard_map.73) | data formatting | bytes 196608

commit v4 on v3

--- a/solution.py
+++ b/solution.py
@@ -25,7 +25,7 @@
 def kernel(
     jac_hbm, panel_hbm, weights_hbm, lists_hbm, masks_hbm, order_hbm, finv_hbm, out,
     jac, panel, weights, lists, masks, order,
-    ws, wk, jm, jx, px, finv, fhi, flo, bd, phi, plo, gy, ysend, yrecv, done,
+    ws, wk, jm, jx, px, finv, fhi, flo, bd, terms_of, gy, ysend, yrecv, done,
     s_in, s_w, s_w0, r_w, s_jz, r_jz, s_pz, r_pz, s_jx, r_jx, s_px, r_px,
     s_h, r_far, r_half, s_sb, r_sb, s_y, r_y, ready,
 ):
@@ -86,20 +86,6 @@
     wcol = jnp.sum(jnp.where(eye, jnp.broadcast_to(weights[...], (ROWS, ROWS)), 0.0), axis=1, keepdims=True)
     for q in range(X):
         ws[q] = (wcol * panel[:, q * Q : (q + 1) * Q].astype(F32)).astype(BF16)
-
-    for copy in inputs[2:5]:
-        copy.wait()
-    lane = lax.broadcasted_iota(jnp.int32, (1, 128), 1)
-    ids = order[...]
-    place = lax.broadcasted_iota(jnp.int32, (1, NT), 1).astype(F32) + 1.0
-    base = (zh % 4) * SL + x * NB
-    note = jnp.zeros((1, 128), F32)
-    for b in range(NB):
-        for k in range(KT):
-            hit = jnp.sum(jnp.where(ids == lists[b, k], place, 0.0), axis=1, keepdims=True)
-            hit = hit * masks[b, k].astype(F32)
-            note = note + jnp.where(lane == base + k * BT + b, hit, 0.0)
-    px[x, zh] = note
 
     pl.semaphore_wait(barrier, 5 * (X - 1) + ZH - 1 + Y - 1)
 
@@ -140,6 +126,20 @@
 
     spread(0)
 
+    for copy in inputs[2:5]:
+        copy.wait()
+    lane = lax.broadcasted_iota(jnp.int32, (1, 128), 1)
+    ids = order[...]
+    place = lax.broadcasted_iota(jnp.int32, (1, NT), 1).astype(F32) + 1.0
+    base = (zh % 4) * SL + x * NB
+    note = jnp.zeros((1, 128), F32)
+    for b in range(NB):
+        for k in range(KT):
+            hit = jnp.sum(jnp.where(ids == lists[b, k], place, 0.0), axis=1, keepdims=True)
+            hit = hit * masks[b, k].astype(F32)
+            note = note + jnp.where(lane == base + k * BT + b, hit, 0.0)
+    px[x, zh] = note
+
     def tell(d, carry):
         send(px.at[x, zh], px.at[x, zh], s_pz, r_pz, at_zh(d))
         return carry
@@ -155,7 +155,7 @@
         jx[half, x, zh] = jm[half, zh]
 
     inputs[6].wait()
-    full = finv[...]
+    full = finv[...].T
     high = full.astype(BF16)
     fhi[...] = high
     flo[...] = (full - high.astype(F32)).astype(BF16)
@@ -237,8 +237,8 @@
         top = terms.astype(BF16)
         rest = (terms - top.astype(F32)).astype(BF16)
         where = pl.ds(pl.multiple_of(t * SL, SL), SL)
-        phi[half * M8 : (half + 1) * M8, where, :] = top.reshape(M8, SL, Q)
-        plo[half * M8 : (half + 1) * M8, where, :] = rest.reshape(M8, SL, Q)
+        both = jnp.concatenate([top, rest], axis=1)
+        terms_of[half * M8 : (half + 1) * M8, where, :] = both.reshape(M8, SL, 2 * Q)
 
     def lay_out_pair(half):
         def one(i, carry):
@@ -289,17 +289,19 @@
 
     for half in range(YH):
         if half == 0:
-            lax.fori_loop(close, Z, products(0), 0)
+            for i in range(close, Z):
+                product(0, distance(i) * H + h)
+            for i in range(close, Z):
+                arrived(wk.at[0], r_sb.at[distance(i)])
+                product(0, distance(i) * H + (1 - h))
         else:
             lax.fori_loop(0, Z, lay_out_pair(1), 0)
             lax.fori_loop(0, Z, products(1), 0)
         for up in range(YH):
             for m in range(M4):
                 here = half * M8 + up * M4 + m
-                gram = jnp.dot(chosen, phi[here], preferred_element_type=F32) + jnp.dot(
-                    chosen, plo[here], preferred_element_type=F32
-                )
-                gy[up, m * NT : (m + 1) * NT, :] = gram
+                gram = jnp.dot(chosen, terms_of[here], preferred_element_type=F32)
+                gy[up, m * NT : (m + 1) * NT, :] = gram[:, :Q] + gram[:, Q:]
             for c in range(YL * X):
                 ysend[half, up * YL * X + c] = gy[up, pl.ds(c, M4 * PER, stride=YL * X), :].astype(BF16)
 
@@ -328,10 +330,9 @@
     ghi = gram.astype(BF16)
     glo = (gram - ghi.astype(F32)).astype(BF16)
 
-    def times(a, b):
-        return lax.dot_general(a, b[...], (((1,), (1,)), ((), ())), preferred_element_type=F32)
-
-    out[...] = (times(ghi, fhi) + (times(ghi, flo) + times(glo, fhi))).reshape(PER, M8, PANEL)
+    wide = jnp.dot(jnp.concatenate([ghi, glo], axis=0), fhi[...], preferred_element_type=F32)
+    low = jnp.dot(ghi, flo[...], preferred_element_type=F32)
+    out[...] = (wide[: PER * M8] + (wide[PER * M8 :] + low)).reshape(PER, M8, PANEL)
 
     arrived(wk.at[pl.ds(0, 4)], s_w)
     arrived(wk.at[0, pl.ds(0, X - 1)], s_w0)
@@ -371,8 +372,7 @@
             pltpu.VMEM((PANEL, PANEL), BF16),
             pltpu.VMEM((PANEL, PANEL), BF16),
             pltpu.VMEM((ZH, M * SL, X * ROWS), BF16),
-            pltpu.VMEM((M, ZH * SL, Q), BF16),
-            pltpu.VMEM((M, ZH * SL, Q), BF16),
+            pltpu.VMEM((M, ZH * SL, 2 * Q), BF16),
             pltpu.VMEM((YH, M4 * NT, Q), F32),
             pltpu.VMEM((2, Y * X, M4 * PER, Q), BF16),
             pltpu.VMEM((2, Y * X, M4 * PER, Q), BF16),

time: 46.6 us -> 45.8 us (0.983)
  Pallas kernels: 45.9 us -> 45 us
    pallas_call x1, Pallas kernels: 45.9 us -> 45 us  [local(): pl.pallas_call(kernel, out_shape=jax.ShapeDtypeStruct((PER, M8, PANEL), F...]
where the time goes in v4:
time: 45.8 us; the launch traced here: 45.7 us
  Pallas kernels  45 us (98%)
  local copies, waits for them, and re-layouts  0.64 us (1%)
    pallas_call x1, Pallas kernels, local(): pl.pallas_call(kernel, out_shape=jax.ShapeDtypeStruct((PER, M8, PANEL), F...  45 us

profile of v4, /device:TPU:1, one launch (start us, length us, event | category | flops | bytes accessed | tf_op | source)
XLA Modules:
  0.0 45.7 jit_solution(938699077488501104)
XLA Ops:
  0.0 45.0 %shard_map.73 = f32[6,8,512]{2,1,0:T(8,128)S(1)} custom-call(bf16[64,1024]{1,0:T(8,128)(2,1)} %jac_hbm.1, bf16[64,512]{1,0:T(8,128)(2,1)} %panel_hbm.1, f32[1,64]{1,0:T(1,128)} %bitcast.2, s32[2,4]{1,0:T(2,128)} %lists_hbm.1, s32[2,4]{1,0:T(2,128)} %masks_hbm.1, s32[1,96]{1,0:T(1,128)} %bitcast.3, f32[512,512]{1,0:T(8,128)} %finv_hbm.1), custom_call_target="tpu_custom_call" | custom-call | tf_op jit(solution)/shard_map/pallas_call | solution.py:354
  45.0 0.6 %copy.9 = f32[6,8,512]{2,1,0:T(8,128)} copy(f32[6,8,512]{2,1,0:T(8,128)S(1)} %shard_map.73) | data formatting | bytes 196608

commit v5 on v4

--- a/solution.py
+++ b/solution.py
@@ -313,7 +313,9 @@
             )
             return carry
 
-        lax.fori_loop(1, Y * X, deliver, 0)
+        for turn in (4, 3, 5, 2, 6, 1, 7):
+            lax.fori_loop(turn * X, turn * X + X, deliver, 0)
+        lax.fori_loop(1, X, deliver, 0)
         yrecv[half, y * X + x] = ysend[half, y * X + x]
 
     for half in range(2):

time: 45.8 us -> 45 us (0.983)
  Pallas kernels: 45 us -> 44.3 us
    pallas_call x1, Pallas kernels: 45 us -> 44.3 us  [local(): pl.pallas_call(kernel, out_shape=jax.ShapeDtypeStruct((PER, M8, PANEL), F...]
where the time goes in v5:
time: 45 us; the launch traced here: 44.9 us
  Pallas kernels  44.3 us (98%)
  local copies, waits for them, and re-layouts  0.64 us (1%)
    pallas_call x1, Pallas kernels, local(): pl.pallas_call(kernel, out_shape=jax.ShapeDtypeStruct((PER, M8, PANEL), F...  44.3 us

profile of v5, /device:TPU:1, one launch (start us, length us, event | category | flops | bytes accessed | tf_op | source)
XLA Modules:
  0.0 44.9 jit_solution(4919827707002256927)
XLA Ops:
  0.0 44.3 %shard_map.73 = f32[6,8,512]{2,1,0:T(8,128)S(1)} custom-call(bf16[64,1024]{1,0:T(8,128)(2,1)} %jac_hbm.1, bf16[64,512]{1,0:T(8,128)(2,1)} %panel_hbm.1, f32[1,64]{1,0:T(1,128)} %bitcast.2, s32[2,4]{1,0:T(2,128)} %lists_hbm.1, s32[2,4]{1,0:T(2,128)} %masks_hbm.1, s32[1,96]{1,0:T(1,128)} %bitcast.3, f32[512,512]{1,0:T(8,128)} %finv_hbm.1), custom_call_target="tpu_custom_call" | custom-call | tf_op jit(solution)/shard_map/pallas_call | solution.py:356
  44.3 0.6 %copy.9 = f32[6,8,512]{2,1,0:T(8,128)} copy(f32[6,8,512]{2,1,0:T(8,128)S(1)} %shard_map.73) | data formatting | bytes 196608

commit v6 on v5

--- a/solution.py
+++ b/solution.py
@@ -296,7 +296,8 @@
                 product(0, distance(i) * H + (1 - h))
         else:
             lax.fori_loop(0, Z, lay_out_pair(1), 0)
-            lax.fori_loop(0, Z, products(1), 0)
+            for i in range(Z):
+                products(1)(i, 0)
         for up in range(YH):
             for m in range(M4):
                 here = half * M8 + up * M4 + m

time: 45 us -> 44.8 us (level)
  no operation moved by 1% of the time
where the time goes in v6:
time: 44.8 us; the launch traced here: 44.7 us
  Pallas kernels  44.1 us (98%)
  local copies, waits for them, and re-layouts  0.64 us (1%)
    pallas_call x1, Pallas kernels, local(): pl.pallas_call(kernel, out_shape=jax.ShapeDtypeStruct((PER, M8, PANEL), F...  44.1 us

profile of v6, /device:TPU:1, one launch (start us, length us, event | category | flops | bytes accessed | tf_op | source)
XLA Modules:
  0.0 44.7 jit_solution(15611257468380973465)
XLA Ops:
  0.0 44.1 %shard_map.73 = f32[6,8,512]{2,1,0:T(8,128)S(1)} custom-call(bf16[64,1024]{1,0:T(8,128)(2,1)} %jac_hbm.1, bf16[64,512]{1,0:T(8,128)(2,1)} %panel_hbm.1, f32[1,64]{1,0:T(1,128)} %bitcast.2, s32[2,4]{1,0:T(2,128)} %lists_hbm.1, s32[2,4]{1,0:T(2,128)} %masks_hbm.1, s32[1,96]{1,0:T(1,128)} %bitcast.3, f32[512,512]{1,0:T(8,128)} %finv_hbm.1), custom_call_target="tpu_custom_call" | custom-call | tf_op jit(solution)/shard_map/pallas_call | solution.py:357
  44.1 0.6 %copy.9 = f32[6,8,512]{2,1,0:T(8,128)} copy(f32[6,8,512]{2,1,0:T(8,128)S(1)} %shard_map.73) | data formatting | bytes 196608
